TPU v7x, 32 devices: a whole 2x2x4 slice. The times are simulated.
32 devices in a mesh: dp: 8 (over z, x), tensor: 4 (over y, core).
Axes of the slice: x: 2, y: 2, z: 4, core: 2. Of those that a mesh axis runs over, the one named last changes fastest.
Arguments:
- tokens: bfloat16 [32768, 768], P(('dp', 'tensor')), may hold values from -6 to 6
- cotangent: bfloat16 [32768, 768], P(('dp', 'tensor')), may hold values from -26 to 26
- seq_group: int32 [16], P('dp'), may hold values from 0 to 1
- block_slot: int32 [13830], replicated, may hold values from 0 to 20751, as said below
- master: float32 [4, 20752, 128], P('tensor', 'dp'), may hold values from -3 to 3
- first_moment: float32 [4, 20752, 128], P('tensor', 'dp'), may hold values from -1 to 1
- second_moment: float32 [4, 20752, 128], P('tensor', 'dp'), may hold values from 0 to 1, as said below
Outputs:
- output: bfloat16 [32768, 768], P(('dp', 'tensor'))
- input_grad: float32 [32768, 768], P(('dp', 'tensor'))
- group_norms: float32 [16], P('dp')
- new_master: float32 [4, 20752, 128], P('tensor', 'dp')
- new_first: float32 [4, 20752, 128], P('tensor', 'dp')
- new_second: float32 [4, 20752, 128], P('tensor', 'dp')
Inputs may be any that keep to these rules, and one draw needn't show every extreme that they name: `block_slot`: all entries differ; slot s belongs to the owner with dp index s // 2594; one owner holds 2594 blocks. `seq_group`: group ids count within one dp index: sequences of different dp indices never share a group. `second_moment`: Positive.
All inputs are finite; a program needn't handle non-finite values.
Results may differ from a plain program's by a relative error of at most 0.012.
Values may be sent and summed in bfloat16 or wider, within the bound.
No kernel may reach another device: no remote copies, remote signals or barrier semaphores. Data moves between devices by JAX's collectives and lax.ppermute only.
A program may use at most 256 MiB of HBM per device.

v0:
```python
import jax
import jax.numpy as jnp
from jax import lax
from jax.sharding import PartitionSpec as P

HEADS = 12
HD = 64
ROT = 16
FF = 3072
eps_norm = 1e-05
eps_adam = 1e-08
beta_one = 0.5
beta_two = 0.6
root_half = 0.7071067811865476
inv_root_tau = 0.3989422804014327


def rotary_tables(length, rot_dims):
    half_rot = rot_dims // 2
    frequency = 10000.0 ** (-2.0 * jnp.arange(half_rot, dtype=jnp.float32) / rot_dims)
    angles = jnp.arange(length, dtype=jnp.float32)[:, None] * frequency[None, :]
    return (jnp.cos(angles), jnp.sin(angles))


def rotate(features, cosine, sine_table, rot_dims):
    half_rot = rot_dims // 2
    first_half = features[..., :half_rot]
    second_half = features[..., half_rot:rot_dims]
    cos_cols = cosine[:, None, :]
    sin_cols = sine_table[:, None, :]
    return jnp.concatenate(
        [
            first_half * cos_cols - second_half * sin_cols,
            second_half * cos_cols + first_half * sin_cols,
            features[..., rot_dims:],
        ],
        axis=-1,
    )


def unrotate(grad_in, cosine, sine_table, rot_dims):
    half_rot = rot_dims // 2
    first_half = grad_in[..., :half_rot]
    second_half = grad_in[..., half_rot:rot_dims]
    cos_cols = cosine[:, None, :]
    sin_cols = sine_table[:, None, :]
    return jnp.concatenate(
        [
            first_half * cos_cols + second_half * sin_cols,
            second_half * cos_cols - first_half * sin_cols,
            grad_in[..., rot_dims:],
        ],
        axis=-1,
    )


def layer_norm(rows_in):
    row_mean = jnp.mean(rows_in, axis=-1, keepdims=True)
    centred = rows_in - row_mean
    inverse = lax.rsqrt(jnp.mean(centred * centred, axis=-1, keepdims=True) + eps_norm)
    return (centred * inverse, inverse)


def unpack(flat_params, d_model, heads_local, ff_local, width_local):
    inner_width = heads_local * HD
    end_qkv = d_model * 3 * inner_width
    end_out = end_qkv + inner_width * d_model
    end_up = end_out + d_model * ff_local
    end_down = end_up + ff_local * d_model
    return (
        flat_params[:end_qkv].reshape(d_model, 3 * inner_width),
        flat_params[end_qkv:end_out].reshape(inner_width, d_model),
        flat_params[end_out:end_up].reshape(d_model, ff_local),
        flat_params[end_up:end_down].reshape(ff_local, d_model),
        flat_params[end_down:].reshape(4, width_local),
    )


def step_rates(position, d_model, heads_local, head_dim, ff_local, seq_len, ff_all):
    end_qkv = d_model * 3 * heads_local * head_dim
    end_out = end_qkv + heads_local * head_dim * d_model
    end_up = end_out + d_model * ff_local
    end_down = end_up + ff_local * d_model
    matrix_rate = d_model ** (-0.5)
    learn_rate = jnp.where(
        position < end_qkv,
        matrix_rate,
        jnp.where(
            position < end_out,
            (seq_len / (5.0 * d_model)) ** 0.5,
            jnp.where(
                position < end_up,
                matrix_rate,
                jnp.where(position < end_down, ff_all ** (-0.5), 0.1),
            ),
        ),
    )
    weight_decay = jnp.where(position < end_down, 0.1, 0.0)
    return (learn_rate.astype(jnp.float32), weight_decay.astype(jnp.float32))


def adam_update(weight, moment_one, moment_two, gradient, learn_rate, weight_decay):
    new_one = beta_one * moment_one + (1.0 - beta_one) * gradient
    new_two = beta_two * moment_two + (1.0 - beta_two) * gradient * gradient
    new_weight = weight - learn_rate * (
        new_one / (jnp.sqrt(new_two) + eps_adam) + weight_decay * weight
    )
    return (new_weight, new_one, new_two)


def by_sequence(tensor_in, seq_count):
    return tensor_in.reshape(seq_count, -1, tensor_in.shape[-1])


def seq_product(left, right, seq_count):
    return jnp.einsum(
        "sli,slj->sij",
        by_sequence(left, seq_count),
        by_sequence(right, seq_count),
        preferred_element_type=jnp.float32,
    )


def on_device(tokens, cotangent, seq_group, block_slot, master, first_moment, second_moment):
    tensor_count = lax.axis_size("tensor")
    tensor_rank = lax.axis_index("tensor")
    owner_index = lax.axis_index("dp")
    owner_count = lax.axis_size("dp")
    d_model = tokens.shape[1]
    local_rows = tokens.shape[0]
    width_local = d_model // tensor_count
    heads_local = HEADS // tensor_count
    inner_width = heads_local * HD
    ff_local = FF // tensor_count
    seq_count = seq_group.shape[0]
    tok_count = local_rows * tensor_count
    seq_len = tok_count // seq_count
    capacity = master.shape[1]
    block_width = master.shape[2]
    block_count = block_slot.shape[0]
    copies = lax.all_gather(master[0].astype(jnp.bfloat16), "dp", axis=0, tiled=True)
    flat_params = copies[block_slot].reshape(-1)
    w_qkv, w_out, w_up, w_down, norm_local = unpack(
        flat_params, d_model, heads_local, ff_local, width_local
    )
    x_full, norm_rows = (
        lax.all_gather(tokens, "tensor", axis=0, tiled=True),
        lax.all_gather(norm_local.reshape(1, 4 * width_local), "tensor", axis=0, tiled=True),
    )
    norm_full = jnp.transpose(norm_rows.reshape(tensor_count, 4, width_local), (1, 0, 2)).reshape(
        4, d_model
    )
    rows_full = x_full.astype(jnp.float32)
    normed, inverse = layer_norm(rows_full)
    norm_gains = norm_full.astype(jnp.float32)
    first_in = (normed * norm_gains[0] + norm_gains[1]).astype(jnp.bfloat16)
    second_in = (normed * norm_gains[2] + norm_gains[3]).astype(jnp.bfloat16)
    projected = jnp.dot(first_in, w_qkv, preferred_element_type=jnp.float32).reshape(
        seq_count, seq_len, 3, heads_local, HD
    )
    cosine, sine_table = rotary_tables(seq_len, ROT)
    queries = rotate(projected[:, :, 0], cosine, sine_table, ROT).astype(jnp.bfloat16)
    key_rows = rotate(projected[:, :, 1], cosine, sine_table, ROT).astype(jnp.bfloat16)
    values = projected[:, :, 2].astype(jnp.bfloat16)
    block_rows = min(512, seq_len)
    block_total = seq_len // block_rows
    scale_factor = HD ** (-0.5)
    starts = jnp.arange(block_total, dtype=jnp.int32) * block_rows
    key_index = jnp.arange(seq_len, dtype=jnp.int32)

    def scores_of(row_start):
        query_block = lax.dynamic_slice_in_dim(queries, row_start, block_rows, 1)
        scores = (
            jnp.einsum("sqhd,skhd->shqk", query_block, key_rows, preferred_element_type=jnp.float32)
            * scale_factor
        )
        allowed = (row_start + jnp.arange(block_rows, dtype=jnp.int32))[:, None] >= key_index[
            None, :
        ]
        return (jnp.where(allowed, scores, -1e30), query_block)

    def forward_block(row_start):
        scores = scores_of(row_start)[0]
        row_peak = jnp.max(scores, axis=-1, keepdims=True)
        exp_scores = jnp.exp(scores - row_peak)
        row_total = jnp.sum(exp_scores, axis=-1, keepdims=True)
        weights_low = (exp_scores / row_total).astype(jnp.bfloat16)
        mixed_heads = jnp.einsum(
            "shqk,skhd->sqhd", weights_low, values, preferred_element_type=jnp.float32
        )
        return (mixed_heads, row_peak + jnp.log(row_total))

    mixed_heads, log_sums = lax.map(forward_block, starts)
    attended = jnp.moveaxis(mixed_heads, 0, 1).reshape(tok_count, inner_width).astype(jnp.bfloat16)
    hidden_pre = jnp.dot(second_in, w_up, preferred_element_type=jnp.float32)
    hidden_low = jax.nn.gelu(hidden_pre, approximate=False).astype(jnp.bfloat16)
    branch = jnp.dot(attended, w_out, preferred_element_type=jnp.float32) + jnp.dot(
        hidden_low, w_down, preferred_element_type=jnp.float32
    )
    branch_sum = lax.psum_scatter(
        branch.astype(jnp.bfloat16), "tensor", scatter_dimension=0, tiled=True
    ).astype(jnp.float32)
    output = (tokens.astype(jnp.float32) + branch_sum).astype(jnp.bfloat16)
    back_full = lax.all_gather(cotangent, "tensor", axis=0, tiled=True)
    grad_down = seq_product(hidden_low, back_full, seq_count)
    grad_hidden = jnp.dot(back_full, w_down.T, preferred_element_type=jnp.float32)
    cumulative = 0.5 * (1.0 + lax.erf(hidden_pre * root_half))
    density = jnp.exp(-0.5 * hidden_pre * hidden_pre) * inv_root_tau
    grad_pre = (grad_hidden * (cumulative + hidden_pre * density)).astype(jnp.bfloat16)
    grad_up = seq_product(second_in, grad_pre, seq_count)
    second_back = jnp.dot(grad_pre, w_up.T, preferred_element_type=jnp.float32)
    grad_out = seq_product(attended, back_full, seq_count)
    grad_attended = jnp.dot(back_full, w_out.T, preferred_element_type=jnp.float32).astype(
        jnp.bfloat16
    )
    grad_blocks_in = jnp.moveaxis(
        grad_attended.reshape(seq_count, block_total, block_rows, heads_local, HD), 1, 0
    )

    def backward_block(carried, inputs):
        row_start, log_sum, grad_block = inputs
        scores, query_block = scores_of(row_start)
        probs = jnp.exp(scores - log_sum)
        grad_probs = jnp.einsum(
            "sqhd,skhd->shqk", grad_block, values, preferred_element_type=jnp.float32
        )
        row_dot = jnp.sum(probs * grad_probs, axis=-1, keepdims=True)
        grad_scores = (probs * (grad_probs - row_dot)).astype(jnp.bfloat16)
        grad_query = (
            jnp.einsum("shqk,skhd->sqhd", grad_scores, key_rows, preferred_element_type=jnp.float32)
            * scale_factor
        )
        grad_keys = (
            carried[0]
            + jnp.einsum(
                "shqk,sqhd->skhd", grad_scores, query_block, preferred_element_type=jnp.float32
            )
            * scale_factor
        )
        grad_values = carried[1] + jnp.einsum(
            "shqk,sqhd->skhd",
            probs.astype(jnp.bfloat16),
            grad_block,
            preferred_element_type=jnp.float32,
        )
        return ((grad_keys, grad_values), grad_query)

    zero_heads = jnp.zeros((seq_count, seq_len, heads_local, HD), jnp.float32)
    key_value_grads, grad_queries = lax.scan(
        backward_block, (zero_heads, zero_heads), (starts, log_sums, grad_blocks_in)
    )
    grad_queries = jnp.moveaxis(grad_queries, 0, 1).reshape(seq_count, seq_len, heads_local, HD)
    grad_qkv = (
        jnp.stack(
            [
                unrotate(grad_queries, cosine, sine_table, ROT),
                unrotate(key_value_grads[0], cosine, sine_table, ROT),
                key_value_grads[1],
            ],
            axis=2,
        )
        .reshape(tok_count, 3 * inner_width)
        .astype(jnp.bfloat16)
    )
    grad_qkv_w = seq_product(first_in, grad_qkv, seq_count)
    first_back = jnp.dot(grad_qkv, w_qkv.T, preferred_element_type=jnp.float32)
    row_start_local = tensor_rank * local_rows
    first_sum, second_sum = (
        lax.psum_scatter(
            first_back.astype(jnp.bfloat16), "tensor", scatter_dimension=0, tiled=True
        ).astype(jnp.float32),
        lax.psum_scatter(
            second_back.astype(jnp.bfloat16), "tensor", scatter_dimension=0, tiled=True
        ).astype(jnp.float32),
    )
    normed_rows = lax.dynamic_slice_in_dim(normed, row_start_local, local_rows, 0)
    inverse_rows = lax.dynamic_slice_in_dim(inverse, row_start_local, local_rows, 0)
    scaled_first = first_sum * norm_gains[0]
    scaled_second = second_sum * norm_gains[2]
    first_mean = jnp.mean(scaled_first, axis=1, keepdims=True)
    first_cross = jnp.mean(scaled_first * normed_rows, axis=1, keepdims=True)
    second_mean = jnp.mean(scaled_second, axis=1, keepdims=True)
    second_cross = jnp.mean(scaled_second * normed_rows, axis=1, keepdims=True)
    grad_input = (
        cotangent.astype(jnp.float32)
        + inverse_rows * (scaled_first - first_mean - normed_rows * first_cross)
        + inverse_rows * (scaled_second - second_mean - normed_rows * second_cross)
    )
    row_seq = (row_start_local + jnp.arange(local_rows, dtype=jnp.int32)) // seq_len
    row_member = (row_seq[None, :] == jnp.arange(seq_count, dtype=jnp.int32)[:, None]).astype(
        jnp.float32
    )
    partial_sums = jnp.stack(
        [
            jnp.dot(row_member, first_sum * normed_rows, precision=lax.Precision.HIGHEST),
            jnp.dot(row_member, first_sum, precision=lax.Precision.HIGHEST),
            jnp.dot(row_member, second_sum * normed_rows, precision=lax.Precision.HIGHEST),
            jnp.dot(row_member, second_sum, precision=lax.Precision.HIGHEST),
        ],
        axis=1,
    )
    norm_grads = lax.psum_scatter(partial_sums, "tensor", scatter_dimension=2, tiled=True)
    per_seq = jnp.concatenate(
        [
            grad_qkv_w.reshape(seq_count, -1),
            grad_out.reshape(seq_count, -1),
            grad_up.reshape(seq_count, -1),
            grad_down.reshape(seq_count, -1),
            norm_grads.reshape(seq_count, -1),
        ],
        axis=1,
    )
    member = (seq_group[None, :] == jnp.arange(seq_count, dtype=jnp.int32)[:, None]).astype(
        jnp.float32
    )
    group_grads = jnp.dot(member, per_seq, precision=lax.Precision.HIGHEST)
    squares = lax.psum(jnp.sum(group_grads * group_grads, axis=1), "tensor")
    group_norms = jnp.sqrt(squares)
    clip_scale = 1.0 / jnp.maximum(group_norms, 1.0)
    clipped = jnp.dot(clip_scale, group_grads, precision=lax.Precision.HIGHEST)
    grad_rows = clipped.reshape(block_count, block_width)
    slot_total = owner_count * capacity
    slot_block = (
        jnp.full((slot_total,), -1, jnp.int32)
        .at[block_slot]
        .set(jnp.arange(block_count, dtype=jnp.int32))
    )
    my_blocks = lax.dynamic_slice_in_dim(slot_block, owner_index * capacity, capacity)
    summed = lax.psum(grad_rows, "dp")
    owned_grad = jnp.where(my_blocks[:, None] >= 0, summed[jnp.maximum(my_blocks, 0)], 0.0)
    position = (
        jnp.maximum(my_blocks, 0)[:, None] * block_width
        + jnp.arange(block_width, dtype=jnp.int32)[None, :]
    )
    learn_rate, weight_decay = step_rates(position, d_model, heads_local, HD, ff_local, seq_len, FF)
    new_weight, new_one, new_two = adam_update(
        master[0], first_moment[0], second_moment[0], owned_grad, learn_rate, weight_decay
    )
    return (output, grad_input, group_norms, new_weight[None], new_one[None], new_two[None])


def solution(mesh):
    placed = (
        P(("dp", "tensor"), None),
        P(("dp", "tensor"), None),
        P("dp"),
        P(),
        P("tensor", "dp", None),
        P("tensor", "dp", None),
        P("tensor", "dp", None),
    )
    return jax.shard_map(
        on_device,
        mesh=mesh,
        in_specs=placed,
        out_specs=(
            P(("dp", "tensor"), None),
            P(("dp", "tensor"), None),
            P("dp"),
            P("tensor", "dp", None),
            P("tensor", "dp", None),
            P("tensor", "dp", None),
        ),
        check_vma=False,
    )
```

profile of v0, /device:TPU:0, one launch (start us, length us, event | category | flops | bytes accessed | tf_op | source)
XLA Modules:
  0.0 1451.3 jit_solution(10674566761597092681)
XLA Ops:
  17.1 148.8 %all-gather.10.cloned.1.call-done = bf16[1,20752,128]{2,0,1:T(2,128)(2,1)} async-done(((bf16[1,2594,128]{2,0,1:T(2,128)(2,1)}), bf16[1,20752,128]{2,0,1:T(2,128)(2,1)}) %all-gather.10.cloned.1.call-update) | async-done | bytes 5312528 | tf_op jit(solution)/shard_map/all_gather | solution.py:141
  174.4 30.7 %gather_fusion = bf16[13830,128]{1,0:T(8,128)(2,1)S(1)} fusion(bf16[20752,128]{1,0:T(8,128)(2,1)} %bitcast.203, s32[14336]{0:T(1024)} %pad_clamp_fusion), kind=kCustom, calls=%fused_computation | custom fusion | bytes 7136280 | tf_op jit(solution)/shard_map/gather | solution.py:142
  276.1 163.2 %while.30 = (s32[]{:T(128)}, bf16[4,2,512,3,64]{2,4,3,1,0:T(8,128)(2,1)}, f32[4,2,3,512,1]{3,2,1,4,0:T(4,128)S(1)}, s32[4]{0:T(128)S(1)}, bf16[2,2048,3,64]{1,3,...) while((s32[]{:T(128)}, ...), condition=%wide.region_5.6_spmd.clone.clone, body=%wide.region_2.5_spmd.clone.sunk.clone | while | flops 1687156224 | bytes 96723152 | solution.py:193
  361.6 12.1 fusion.178
  439.3 336.2 %while.31 = (s32[]{:T(128)}, f32[2,2048,3,64]{1,3,2,0:T(8,128)}, f32[2,2048,3,64]{1,3,2,0:T(8,128)}, f32[4,2,512,3,64]{2,4,3,1,0:T(8,128)}, s32[4]{0:T(128)S(1)}...) while((s32[]{:T(128)}, f32[2,2048,3,64]{1,3,2,0:T(8,128)}, ...), condition=%wide.region_9.10_spmd.clone.clone, body=%wide.region_7.9_spmd.clone.sunk.clone | while | flops 4126078464 | bytes 275603712 | solution.py:249
  454.8 12.9 bitcast_add_fusion.7
  467.7 18.1 %multiply_reduce_fusion.4 = (f32[2,3,512]{2,1,0:T(4,128)S(1)}, f32[2,3,512,2048]{3,2,1,0:T(8,128)}) fusion(f32[2,3,512,2048]{3,2,1,0:T(8,128)} %fusion.190, f32[2,3,512]{2,1,0:T(4,128)S(1)} %dynamic-slice_bitcast_fusion.3, pred[512,2048]{1,0:T(8,128)(4,1)S(1)} %iota_compare_fusion.12, bf16[2,2048,3,64]{1,3,2,0:T(8,128)(2,1)} %copy-done.1, ...), kind=kOutput, calls=%fused_computation.22.clone.1.clone | convolution fusion | flops 836760576 | bytes 53370884 | tf_op jit(solution)/shard_map/while/body/eval_jaxpr/sqhd,skhd->shqk/dot_general | solution.py:224
  485.8 17.0 %multiply_convert_fusion.3 = bf16[2,3,512,2048]{3,2,1,0:T(8,128)(2,1)S(1)} fusion(f32[2,3,512,2048]{3,2,1,0:T(8,128)} %get-tuple-element.409, f32[2,3,512,2048]{3,2,1,0:T(8,128)} %fusion.190, f32[2,3,512]{2,1,0:T(4,128)S(1)} %get-tuple-element.410, f32[2,3,512]{2,1,0:T(4,128)S(1)} %dynamic-slice_bitcast_fusion.3, ...), kind=kLoop, calls=%fused_computation.21.clone.1.clone | loop fusion | flops 37748736 | bytes 63987712 | tf_op jit(solution)/shard_map/while/body/eval_jaxpr/convert_element_type | solution.py:228
  537.3 13.8 bitcast_add_fusion.7
  551.1 18.1 %multiply_reduce_fusion.4 = (f32[2,3,512]{2,1,0:T(4,128)S(1)}, f32[2,3,512,2048]{3,2,1,0:T(8,128)}) fusion(f32[2,3,512,2048]{3,2,1,0:T(8,128)} %fusion.190, f32[2,3,512]{2,1,0:T(4,128)S(1)} %dynamic-slice_bitcast_fusion.3, pred[512,2048]{1,0:T(8,128)(4,1)S(1)} %iota_compare_fusion.12, bf16[2,2048,3,64]{1,3,2,0:T(8,128)(2,1)} %copy-done.1, ...), kind=kOutput, calls=%fused_computation.22.clone.1.clone | convolution fusion | flops 836760576 | bytes 53370884 | tf_op jit(solution)/shard_map/while/body/eval_jaxpr/sqhd,skhd->shqk/dot_general | solution.py:224
  569.2 17.0 %multiply_convert_fusion.3 = bf16[2,3,512,2048]{3,2,1,0:T(8,128)(2,1)S(1)} fusion(f32[2,3,512,2048]{3,2,1,0:T(8,128)} %get-tuple-element.409, f32[2,3,512,2048]{3,2,1,0:T(8,128)} %fusion.190, f32[2,3,512]{2,1,0:T(4,128)S(1)} %get-tuple-element.410, f32[2,3,512]{2,1,0:T(4,128)S(1)} %dynamic-slice_bitcast_fusion.3, ...), kind=kLoop, calls=%fused_computation.21.clone.1.clone | loop fusion | flops 37748736 | bytes 63987712 | tf_op jit(solution)/shard_map/while/body/eval_jaxpr/convert_element_type | solution.py:228
  621.7 13.8 bitcast_add_fusion.7
  635.5 18.1 %multiply_reduce_fusion.4 = (f32[2,3,512]{2,1,0:T(4,128)S(1)}, f32[2,3,512,2048]{3,2,1,0:T(8,128)}) fusion(f32[2,3,512,2048]{3,2,1,0:T(8,128)} %fusion.190, f32[2,3,512]{2,1,0:T(4,128)S(1)} %dynamic-slice_bitcast_fusion.3, pred[512,2048]{1,0:T(8,128)(4,1)S(1)} %iota_compare_fusion.12, bf16[2,2048,3,64]{1,3,2,0:T(8,128)(2,1)} %copy-done.1, ...), kind=kOutput, calls=%fused_computation.22.clone.1.clone | convolution fusion | flops 836760576 | bytes 53370884 | tf_op jit(solution)/shard_map/while/body/eval_jaxpr/sqhd,skhd->shqk/dot_general | solution.py:224
  653.6 17.0 %multiply_convert_fusion.3 = bf16[2,3,512,2048]{3,2,1,0:T(8,128)(2,1)S(1)} fusion(f32[2,3,512,2048]{3,2,1,0:T(8,128)} %get-tuple-element.409, f32[2,3,512,2048]{3,2,1,0:T(8,128)} %fusion.190, f32[2,3,512]{2,1,0:T(4,128)S(1)} %get-tuple-element.410, f32[2,3,512]{2,1,0:T(4,128)S(1)} %dynamic-slice_bitcast_fusion.3, ...), kind=kLoop, calls=%fused_computation.21.clone.1.clone | loop fusion | flops 37748736 | bytes 63987712 | tf_op jit(solution)/shard_map/while/body/eval_jaxpr/convert_element_type | solution.py:228
  706.1 13.8 bitcast_add_fusion.7
  719.9 18.1 %multiply_reduce_fusion.4 = (f32[2,3,512]{2,1,0:T(4,128)S(1)}, f32[2,3,512,2048]{3,2,1,0:T(8,128)}) fusion(f32[2,3,512,2048]{3,2,1,0:T(8,128)} %fusion.190, f32[2,3,512]{2,1,0:T(4,128)S(1)} %dynamic-slice_bitcast_fusion.3, pred[512,2048]{1,0:T(8,128)(4,1)S(1)} %iota_compare_fusion.12, bf16[2,2048,3,64]{1,3,2,0:T(8,128)(2,1)} %copy-done.1, ...), kind=kOutput, calls=%fused_computation.22.clone.1.clone | convolution fusion | flops 836760576 | bytes 53370884 | tf_op jit(solution)/shard_map/while/body/eval_jaxpr/sqhd,skhd->shqk/dot_general | solution.py:224
  738.0 17.0 %multiply_convert_fusion.3 = bf16[2,3,512,2048]{3,2,1,0:T(8,128)(2,1)S(1)} fusion(f32[2,3,512,2048]{3,2,1,0:T(8,128)} %get-tuple-element.409, f32[2,3,512,2048]{3,2,1,0:T(8,128)} %fusion.190, f32[2,3,512]{2,1,0:T(4,128)S(1)} %get-tuple-element.410, f32[2,3,512]{2,1,0:T(4,128)S(1)} %dynamic-slice_bitcast_fusion.3, ...), kind=kLoop, calls=%fused_computation.21.clone.1.clone | loop fusion | flops 37748736 | bytes 63987712 | tf_op jit(solution)/shard_map/while/body/eval_jaxpr/convert_element_type | solution.py:228
  840.7 33.3 %fusion.41 = (bf16[4096,768]{1,0:T(8,128)(2,1)}, f32[4096,768]{1,0:T(8,128)S(1)}) fusion(bf16[4096,768]{1,0:T(8,128)(2,1)} %get-tuple-element.243, bf16[768,768]{1,0:T(8,128)(2,1)S(1)} %copy-done.22), kind=kOutput, calls=%fused_computation.59 | convolution fusion | flops 5036310528 | bytes 26345472 | tf_op jit(solution)/shard_map/dot_general | solution.py:195
  917.7 12.2 convolution_bitcast_fusion
  946.8 21.3 %reduce-scatter.11.cloned.1.call-done = bf16[1024,768]{1,0:T(8,128)(2,1)} async-done(((bf16[4096,768]{1,0:T(8,128)(2,1)}), bf16[1024,768]{1,0:T(8,128)(2,1)}) %reduce-scatter.11.cloned.1.call-update) | async-done | bytes 1572880 | tf_op jit(solution)/shard_map/reduce_scatter | solution.py:272
  1002.3 41.5 %multiply_reduce_fusion.1 = (f32[2]{0:T(128)S(1)}, f32[2,1770240]{1,0:T(2,128)}) fusion(f32[2,1770240]{1,0:T(2,128)} %constant_dynamic-update-slice_fusion, s32[2]{0:T(128)S(1)} %copy-done.37), kind=kOutput, calls=%fused_computation.55 | convolution fusion | flops 92052480 | bytes 28323856 | tf_op jit(solution)/shard_map/dot_general | solution.py:316
  1050.1 119.3 %convolution_reduce_fusion = f32[1770240]{0:T(1024)} fusion(f32[2,1770240]{1,0:T(2,128)} %get-tuple-element.263, f32[2]{0:T(128)S(1)} %sqrt.7), kind=kOutput, calls=%fused_computation.116 | convolution fusion | flops 42485764 | bytes 21242888 | tf_op jit(solution)/shard_map/dot_general | solution.py:320
  1169.4 65.6 %scatter_custom_fusion = s32[20752]{0:T(1024)S(1)} fusion(s32[13830]{0:T(1024)} %copy-done.27, s32[13830]{0:T(1024)S(1)} %iota.92, s32[]{:T(128)} %constant.72.clone.1), kind=kCustom, calls=%fused_computation.158 | custom fusion | bytes 83520 | tf_op jit(solution)/shard_map/scatter | solution.py:326
  1246.7 157.5 %all-reduce.2.cloned.1.call-done = f32[13830,128]{1,0:T(8,128)} async-done(((f32[13830,128]{1,0:T(8,128)}), f32[13830,128]{1,0:T(8,128)}) %all-reduce.2.cloned.1.call-update) | async-done | bytes 7080976 | tf_op jit(solution)/shard_map/psum | solution.py:329
  (310 shorter events, 582.5 us)
Async XLA Ops:
  7.2 158.7 %all-gather.10.cloned.1.call-start = ((), (), s32[]{:S(2)}) async-start(), calls=%async_computation.10 | async-start | bytes 11953152 | tf_op jit(solution)/shard_map/all_gather | solution.py:141
  10.8 217.5 %all-gather.6.cloned.1.call-start = ((), (), s32[]{:S(2)}) async-start(), calls=%async_computation.4 | async-start | bytes 7864320 | tf_op jit(solution)/shard_map/all_gather | solution.py:147
  11.6 248.4 %all-gather.8.cloned.1.call-start = ((), (), s32[]{:S(2)}) async-start(), calls=%async_computation.6 | async-start | bytes 7864320 | tf_op jit(solution)/shard_map/all_gather | solution.py:204
  12.3 929.1 %reduce-scatter.9.cloned.1.call-start = ((), (), s32[]{:S(2)}) async-start(), calls=%async_computation.7 | async-start | bytes 7864320 | tf_op jit(solution)/shard_map/reduce_scatter | solution.py:269
  214.3 20.6 %copy-start.31 = (f32[768]{0:T(1024)}, f32[768]{0:T(1024)S(1)}, u32[]{:S(2)}) copy-start(f32[768]{0:T(1024)S(1)} %mul.459) | copy-start | bytes 9220
  214.4 20.5 %copy-start.33 = (f32[768]{0:T(1024)}, f32[768]{0:T(1024)S(1)}, u32[]{:S(2)}) copy-start(f32[768]{0:T(1024)S(1)} %mul.475) | copy-start | bytes 9220
  246.9 13.1 copy-start.18
  292.1 12.1 copy-start.7
  332.9 12.1 copy-start.7
  373.7 12.1 copy-start.7
  838.3 129.8 %reduce-scatter.11.cloned.1.call-start = ((), (), s32[]{:S(2)}) async-start(), calls=%async_computation.8 | async-start | bytes 7864320 | tf_op jit(solution)/shard_map/reduce_scatter | solution.py:272
  838.3 35.7 %slice-start.2 = ((s8[6291456]{0:T(1024)(128)(4,1)}), s8[4194304]{0:T(1024)(128)(4,1)S(1)}, s32[]{:S(2)}) async-start(s8[6291456]{0:T(1024)(128)(4,1)} %bitcast.218), calls=%async_computation.14 | async-start | bytes 8388608
  840.6 33.3 %slice-start.3 = ((s8[6291456]{0:T(1024)(128)(4,1)}), s8[2097152]{0:T(1024)(128)(4,1)S(1)}, s32[]{:S(2)}) async-start(s8[6291456]{0:T(1024)(128)(4,1)} %bitcast.218), calls=%async_computation.15 | async-start | bytes 4194304
  840.7 33.3 %copy-start.20 = (bf16[768,768]{1,0:T(8,128)(2,1)S(1)}, bf16[768,768]{1,0:T(8,128)(2,1)}, u32[]{:S(2)}) copy-start(bf16[768,768]{1,0:T(8,128)(2,1)} %reshape.377) | copy-start | bytes 3538948
  909.1 91.2 %reduce-scatter.13.cloned.1.call-start = ((), (), s32[]{:S(2)}) async-start(), calls=%async_computation.11 | async-start | bytes 491520
  917.7 12.2 copy-start.21
  946.8 30.2 %copy-start.19 = (bf16[192,768]{1,0:T(8,128)(2,1)S(1)}, bf16[192,768]{1,0:T(8,128)(2,1)}, u32[]{:S(2)}) copy-start(bf16[192,768]{1,0:T(8,128)(2,1)} %reshape.375) | copy-start | bytes 884740
  976.5 262.1 %reduce-scatter.7.cloned.1.call-start = ((), (), s32[]{:S(2)}) async-start(), calls=%async_computation.5 | async-start | bytes 7864320 | tf_op jit(solution)/shard_map/reduce_scatter | solution.py:200
  994.2 410.0 %all-reduce.2.cloned.1.call-start = ((), (), s32[]{:S(2)}) async-start(), calls=%async_computation.9 | async-start | bytes 14163968 | tf_op jit(solution)/shard_map/psum | solution.py:329
  1050.1 119.3 %copy-start.40 = (f32[2]{0:T(128)}, f32[2]{0:T(128)S(1)}, u32[]{:S(2)}) copy-start(f32[2]{0:T(128)S(1)} %sqrt.7) | copy-start | bytes 28
  1169.4 65.9 %copy-start.5 = (bf16[1024,768]{1,0:T(8,128)(2,1)S(1)}, bf16[1024,768]{1,0:T(8,128)(2,1)}, u32[]{:S(2)}) copy-start(bf16[1024,768]{1,0:T(8,128)(2,1)} %reduce-scatter.9.cloned.1.call-done) | copy-start | bytes 4718596
  1169.4 65.9 %copy-start.32 = (f32[768]{0:T(1024)S(1)}, f32[768]{0:T(1024)}, u32[]{:S(2)}) copy-start(f32[768]{0:T(1024)} %copy-done.31) | copy-start | bytes 9220
  1169.4 65.9 %copy-start.34 = (f32[768]{0:T(1024)S(1)}, f32[768]{0:T(1024)}, u32[]{:S(2)}) copy-start(f32[768]{0:T(1024)} %copy-done.33) | copy-start | bytes 9220
  1246.7 165.3 %copy-start.14 = (f32[1,2594,128]{2,0,1:T(1,128)S(1)}, f32[1,2594,128]{2,0,1:T(1,128)}, u32[]{:S(2)}) copy-start(f32[1,2594,128]{2,0,1:T(1,128)} %param.15) | copy-start | bytes 3984388
  (47 other events, 242.2 us)
Sparse Core Ops, SparseCore 0:
  10.9 154.8 all-gather.9
  167.4 44.5 all-gather.5
  213.6 46.4 all-gather.7
  838.4 58.8 reduce-scatter.8
  909.2 58.8 reduce-scatter.10
  976.7 20.7 reduce-scatter.12
  1000.0 58.9 reduce-scatter.6
  1169.5 234.6 all-reduce.1
where the time goes:
time: 1460 us; the launch traced here: 1450 us
  matrix products  624 us (43%)
  waiting for transfers between devices  339 us (23%)
  local copies, waits for them, and re-layouts  273 us (19%)
  other arithmetic  172 us (12%)
  loops' own time  16.5 us (1%)
  between operations  15.2 us (1%)
    psum x1, waiting for transfers between devices, on_device(): summed = lax.psum(grad_rows, 'dp')  158 us
    all_gather x1, waiting for transfers between devices, on_device(): lax.all_gather(master[0].astype(jnp.bfloat16), 'dp', axis=0, tiled=True)  149 us
    dot_general x1, matrix products, on_device(): clipped = jnp.dot(clip_scale, group_grads, precision=lax.Precision.HIGHEST)  119 us
    dot_general x8, matrix products, scores_of(): jnp.einsum('sqhd,skhd->shqk', query_block, key_rows, preferred_element_ty...  93.7 us
    unnamed x100, local copies, waits for them, and re-layouts  83.8 us
    dot_general x4, matrix products, backward_block(): jnp.einsum('sqhd,skhd->shqk', grad_block, values, preferred_element_type=...  72.5 us
    convert_element_type x4, other arithmetic, backward_block(): grad_scores = (probs * (grad_probs - row_dot)).astype(jnp.bfloat16)  68.2 us
    scatter x1, local copies, waits for them, and re-layouts, on_device(): slot_block = jnp.full((slot_total,), -1, jnp.int32).at[block_slot].set(jn...  65.6 us
  transfers between devices with their start and end apart: 8, of which 4 were waited for; matrix products, arithmetic and copies ran while one was open for 31% of the time, Pallas kernels for 0%

commit v1 on v0

--- a/solution.py
+++ b/solution.py
@@ -2,6 +2,7 @@
 import jax.numpy as jnp
 from jax import lax
 from jax.sharding import PartitionSpec as P
+from jax.lax import all_gather
 
 HEADS = 12
 HD = 64
@@ -326,7 +327,7 @@
         .set(jnp.arange(block_count, dtype=jnp.int32))
     )
     my_blocks = lax.dynamic_slice_in_dim(slot_block, owner_index * capacity, capacity)
-    summed = lax.psum(grad_rows, "dp")
+    summed = jnp.sum(all_gather(grad_rows, "dp"), 0)
     owned_grad = jnp.where(my_blocks[:, None] >= 0, summed[jnp.maximum(my_blocks, 0)], 0.0)
     position = (
         jnp.maximum(my_blocks, 0)[:, None] * block_width

time: 1460 us -> 2320 us (1.59)
  waiting for transfers between devices: 339 us -> 1180 us
    all_gather x0 -> x1, waiting for transfers between devices: none -> 995 us  [on_device(): summed = jnp.sum(all_gather(grad_rows, 'dp'), 0)]
    psum x1 -> x0, waiting for transfers between devices: 158 us -> none  [on_device(): summed = lax.psum(grad_rows, 'dp')]
  transfers between devices with their start and end apart: 8 -> 8, of which waited for: 4 -> 4; matrix products, arithmetic and copies ran while one was open for 31% -> 20% of each run, Pallas kernels for 0% -> 0%
where the time goes in v1:
time: 2320 us; the launch traced here: 2310 us
  waiting for transfers between devices  1180 us (51%)
  matrix products  625 us (27%)
  local copies, waits for them, and re-layouts  273 us (12%)
  other arithmetic  192 us (8%)
    all_gather x1, waiting for transfers between devices, on_device(): summed = jnp.sum(all_gather(grad_rows, 'dp'), 0)  995 us
    all_gather x1, waiting for transfers between devices, on_device(): lax.all_gather(master[0].astype(jnp.bfloat16), 'dp', axis=0, tiled=True)  149 us
    dot_general x1, matrix products, on_device(): clipped = jnp.dot(clip_scale, group_grads, precision=lax.Precision.HIGHEST)  119 us
    dot_general x8, matrix products, scores_of(): jnp.einsum('sqhd,skhd->shqk', query_block, key_rows, preferred_element_ty...  93.7 us
    unnamed x100, local copies, waits for them, and re-layouts  83.8 us
    dot_general x4, matrix products, backward_block(): jnp.einsum('sqhd,skhd->shqk', grad_block, values, preferred_element_type=...  72.5 us
    convert_element_type x4, other arithmetic, backward_block(): grad_scores = (probs * (grad_probs - row_dot)).astype(jnp.bfloat16)  68.2 us
    scatter x1, local copies, waits for them, and re-layouts, on_device(): slot_block = jnp.full((slot_total,), -1, jnp.int32).at[block_slot].set(jn...  65.6 us
  transfers between devices with their start and end apart: 8, of which 4 were waited for; matrix products, arithmetic and copies ran while one was open for 20% of the time, Pallas kernels for 0%

profile of v1, /device:TPU:0, one launch (start us, length us, event | category | flops | bytes accessed | tf_op | source)
XLA Modules:
  0.0 2310.0 jit_solution(8579699420731872991)
XLA Ops:
  17.0 148.9 %all-gather.13.cloned.1.call-done = bf16[1,20752,128]{2,0,1:T(2,128)(2,1)} async-done(((bf16[1,2594,128]{2,0,1:T(2,128)(2,1)}), bf16[1,20752,128]{2,0,1:T(2,128)(2,1)}) %all-gather.13.cloned.1.call-update) | async-done | bytes 5312528 | tf_op jit(solution)/shard_map/all_gather | solution.py:142
  174.4 30.7 %gather_fusion = bf16[13830,128]{1,0:T(8,128)(2,1)S(1)} fusion(bf16[20752,128]{1,0:T(8,128)(2,1)} %bitcast.203, s32[14336]{0:T(1024)} %pad_clamp_fusion), kind=kCustom, calls=%fused_computation | custom fusion | bytes 7136280 | tf_op jit(solution)/shard_map/gather | solution.py:143
  276.1 163.2 %while.30 = (s32[]{:T(128)}, bf16[4,2,512,3,64]{2,4,3,1,0:T(8,128)(2,1)}, f32[4,2,3,512,1]{3,2,1,4,0:T(4,128)S(1)}, s32[4]{0:T(128)S(1)}, bf16[2,2048,3,64]{1,3,...) while((s32[]{:T(128)}, ...), condition=%wide.region_5.6_spmd.clone.clone, body=%wide.region_2.5_spmd.clone.sunk.clone | while | flops 1687156224 | bytes 96723152 | solution.py:194
  439.3 336.4 %while.31 = (s32[]{:T(128)}, f32[2,2048,3,64]{1,3,2,0:T(8,128)}, f32[2,2048,3,64]{1,3,2,0:T(8,128)}, f32[4,2,512,3,64]{2,4,3,1,0:T(8,128)}, s32[4]{0:T(128)S(1)}...) while((s32[]{:T(128)}, f32[2,2048,3,64]{1,3,2,0:T(8,128)}, ...), condition=%wide.region_9.10_spmd.clone.clone, body=%wide.region_7.9_spmd.clone.sunk.clone | while | flops 4126078464 | bytes 275603712 | solution.py:250
  454.8 13.0 bitcast_add_fusion.7
  467.8 18.1 multiply_reduce_fusion.4
  485.9 17.0 multiply_convert_fusion.3
  537.4 13.8 bitcast_add_fusion.7
  551.2 18.1 multiply_reduce_fusion.4
  569.3 17.0 multiply_convert_fusion.3
  621.8 13.8 bitcast_add_fusion.7
  635.7 18.1 multiply_reduce_fusion.4
  653.8 17.0 multiply_convert_fusion.3
  706.2 13.8 bitcast_add_fusion.7
  720.1 18.1 multiply_reduce_fusion.4
  738.2 17.0 multiply_convert_fusion.3
  840.8 33.4 %fusion.41 = (bf16[4096,768]{1,0:T(8,128)(2,1)}, f32[4096,768]{1,0:T(8,128)S(1)}) fusion(bf16[4096,768]{1,0:T(8,128)(2,1)} %get-tuple-element.243, bf16[768,768]{1,0:T(8,128)(2,1)S(1)} %copy-done.22), kind=kOutput, calls=%fused_computation.59 | convolution fusion | flops 5036310528 | bytes 26345472 | tf_op jit(solution)/shard_map/dot_general | solution.py:196
  917.9 12.2 convolution_bitcast_fusion
  946.9 21.3 reduce-scatter.11.cloned.1.call-done
  1002.6 41.5 %multiply_reduce_fusion.1 = (f32[2]{0:T(128)S(1)}, f32[2,1770240]{1,0:T(2,128)}) fusion(f32[2,1770240]{1,0:T(2,128)} %constant_dynamic-update-slice_fusion, s32[2]{0:T(128)S(1)} %copy-done.37), kind=kOutput, calls=%fused_computation.55 | convolution fusion | flops 92052480 | bytes 28323856 | tf_op jit(solution)/shard_map/dot_general | solution.py:317
  1050.4 119.4 %convolution_reduce_fusion = f32[1770240]{0:T(1024)} fusion(f32[2,1770240]{1,0:T(2,128)} %get-tuple-element.263, f32[2]{0:T(128)S(1)} %sqrt.7), kind=kOutput, calls=%fused_computation.116 | convolution fusion | flops 42485764 | bytes 21242888 | tf_op jit(solution)/shard_map/dot_general | solution.py:321
  1169.8 65.6 %scatter_custom_fusion = s32[20752]{0:T(1024)S(1)} fusion(s32[13830]{0:T(1024)} %copy-done.27, s32[13830]{0:T(1024)S(1)} %iota.92, s32[]{:T(128)} %constant.72.clone.1), kind=kCustom, calls=%fused_computation.158 | custom fusion | bytes 83520 | tf_op jit(solution)/shard_map/scatter | solution.py:327
  1246.8 994.9 %all-gather.11.cloned.1.call-done = f32[8,13830,128]{2,1,0:T(8,128)} async-done(((f32[1,13830,128]{2,1,0:T(8,128)}), f32[8,13830,128]{2,1,0:T(8,128)}) %all-gather.11.cloned.1.call-update) | async-done | bytes 56647696 | tf_op jit(solution)/shard_map/all_gather | solution.py:330
  2241.7 21.1 reduce_sum.97
  (311 shorter events, 594.4 us)
Async XLA Ops:
  7.2 158.7 %all-gather.13.cloned.1.call-start = ((), (), s32[]{:S(2)}) async-start(), calls=%async_computation.10 | async-start | bytes 11953152 | tf_op jit(solution)/shard_map/all_gather | solution.py:142
  10.8 217.5 %all-gather.7.cloned.1.call-start = ((), (), s32[]{:S(2)}) async-start(), calls=%async_computation.4 | async-start | bytes 7864320 | tf_op jit(solution)/shard_map/all_gather | solution.py:148
  11.6 248.4 %all-gather.9.cloned.1.call-start = ((), (), s32[]{:S(2)}) async-start(), calls=%async_computation.6 | async-start | bytes 7864320 | tf_op jit(solution)/shard_map/all_gather | solution.py:205
  12.3 929.2 %reduce-scatter.9.cloned.1.call-start = ((), (), s32[]{:S(2)}) async-start(), calls=%async_computation.7 | async-start | bytes 7864320 | tf_op jit(solution)/shard_map/reduce_scatter | solution.py:270
  214.3 20.6 copy-start.31
  214.4 20.6 copy-start.33
  247.0 13.0 copy-start.18
  292.1 12.1 copy-start.7
  332.9 12.1 copy-start.7
  373.7 12.1 copy-start.7
  414.5 12.1 copy-start.7
  838.4 129.8 %reduce-scatter.11.cloned.1.call-start = ((), (), s32[]{:S(2)}) async-start(), calls=%async_computation.8 | async-start | bytes 7864320 | tf_op jit(solution)/shard_map/reduce_scatter | solution.py:273
  838.5 35.7 %slice-start.2 = ((s8[6291456]{0:T(1024)(128)(4,1)}), s8[4194304]{0:T(1024)(128)(4,1)S(1)}, s32[]{:S(2)}) async-start(s8[6291456]{0:T(1024)(128)(4,1)} %bitcast.218), calls=%async_computation.14 | async-start | bytes 8388608
  840.8 33.4 %slice-start.3 = ((s8[6291456]{0:T(1024)(128)(4,1)}), s8[2097152]{0:T(1024)(128)(4,1)S(1)}, s32[]{:S(2)}) async-start(s8[6291456]{0:T(1024)(128)(4,1)} %bitcast.218), calls=%async_computation.15 | async-start | bytes 4194304
  840.8 33.4 %copy-start.20 = (bf16[768,768]{1,0:T(8,128)(2,1)S(1)}, bf16[768,768]{1,0:T(8,128)(2,1)}, u32[]{:S(2)}) copy-start(bf16[768,768]{1,0:T(8,128)(2,1)} %reshape.374) | copy-start | bytes 3538948
  909.2 91.3 %reduce-scatter.13.cloned.1.call-start = ((), (), s32[]{:S(2)}) async-start(), calls=%async_computation.11 | async-start | bytes 491520
  917.9 12.2 copy-start.21
  946.9 30.2 %copy-start.19 = (bf16[192,768]{1,0:T(8,128)(2,1)S(1)}, bf16[192,768]{1,0:T(8,128)(2,1)}, u32[]{:S(2)}) copy-start(bf16[192,768]{1,0:T(8,128)(2,1)} %reshape.372) | copy-start | bytes 884740
  976.7 262.2 %reduce-scatter.7.cloned.1.call-start = ((), (), s32[]{:S(2)}) async-start(), calls=%async_computation.5 | async-start | bytes 7864320 | tf_op jit(solution)/shard_map/reduce_scatter | solution.py:201
  994.5 1247.2 %all-gather.11.cloned.1.call-start = ((), (), s32[]{:S(2)}) async-start(), calls=%async_computation.9 | async-start | bytes 63737856 | tf_op jit(solution)/shard_map/all_gather | solution.py:330
  1050.4 119.4 %copy-start.40 = (f32[2]{0:T(128)}, f32[2]{0:T(128)S(1)}, u32[]{:S(2)}) copy-start(f32[2]{0:T(128)S(1)} %sqrt.7) | copy-start | bytes 28
  1169.8 65.9 %copy-start.5 = (bf16[1024,768]{1,0:T(8,128)(2,1)S(1)}, bf16[1024,768]{1,0:T(8,128)(2,1)}, u32[]{:S(2)}) copy-start(bf16[1024,768]{1,0:T(8,128)(2,1)} %reduce-scatter.9.cloned.1.call-done) | copy-start | bytes 4718596
  1169.8 65.9 %copy-start.32 = (f32[768]{0:T(1024)S(1)}, f32[768]{0:T(1024)}, u32[]{:S(2)}) copy-start(f32[768]{0:T(1024)} %copy-done.31) | copy-start | bytes 9220
  1169.8 65.9 %copy-start.34 = (f32[768]{0:T(1024)S(1)}, f32[768]{0:T(1024)}, u32[]{:S(2)}) copy-start(f32[768]{0:T(1024)} %copy-done.33) | copy-start | bytes 9220
  (47 other events, 237.7 us)
Sparse Core Ops, SparseCore 0:
  10.9 154.8 all-gather.12
  167.4 44.5 all-gather.6
  213.6 46.4 all-gather.8
  838.5 58.8 reduce-scatter.8
  909.3 58.8 reduce-scatter.10
  976.8 20.7 reduce-scatter.12
  1000.2 58.9 reduce-scatter.6
  1169.9 1071.6 all-gather.10
